TPU v7x, 256 devices: a whole 4x4x8 slice. The times are simulated.
256 devices in a mesh: sec: 2 (over core), var: 32 (over y, z), trait: 4 (over x).
Axes of the slice: x: 4, y: 4, z: 8, core: 2. Of those that a mesh axis runs over, the one named last changes fastest.
Arguments:
- z_typed: bfloat16 [262144, 512], P(('sec', 'var'), 'trait'), may hold values from -6 to 6
- band_inverse: bfloat16 [2048, 128, 384], P(('sec', 'var')), may hold values from -0.3125 to 0.3125
- ld_untyped: bfloat16 [4096, 128, 512], P(('sec', 'var')), may hold values from -0.375 to 0.375
- trait_mix: bfloat16 [512, 512], replicated, may hold values from -0.25 to 0.25
- win_start: int32 [4096], P(('sec', 'var')), may hold values from 0 to 2047, as said below
- win_count: int32 [4096], P(('sec', 'var')), may hold values from 1 to 4, as said below
Outputs:
- imputed_mixed: bfloat16 [524288, 512], P(('sec', 'var'), 'trait')
Inputs may be any that keep to these rules, and one draw needn't show every extreme that they name: Windows follow chromosome order: within the 64 untyped blocks of one index g of sec+var, win_start never falls, and every window lies in typed blocks g * 32 - 32 to (g + 1) * 32 + 31; the first window of each index starts at its lower end (or at 0) and the last one ends at its upper end (or at the chromosome's end). win_start + win_count never exceeds 2048.
All inputs are finite; a program needn't handle non-finite values.
Results may differ from a plain program's by a relative error of at most 0.0057.
Values may be sent and summed in bfloat16 or wider, within the bound.
No kernel may reach another device: no remote copies, remote signals or barrier semaphores. Data moves between devices by JAX's collectives and lax.ppermute only.
A program may use at most 64 MiB of HBM per device.

v0:
```python
import jax
import jax.numpy as jnp
from jax import lax
from jax.sharding import PartitionSpec as P

BLK = 128
WIN = 4


def padded_2(cells, sides, width):
    for axis, dim in sides:
        count = lax.axis_size(axis)
        ends = count - 1
        head = lax.slice_in_dim(cells, 0, width, axis=dim)
        tail = lax.slice_in_dim(cells, cells.shape[dim] - width, cells.shape[dim], axis=dim)
        cells = jnp.concatenate(
            [
                lax.ppermute(tail, axis, [(i, (i + 1) % count) for i in range(ends)]),
                cells,
                lax.ppermute(head, axis, [((i + 1) % count, i) for i in range(ends)]),
            ],
            axis=dim,
        )
    return cells


def on_device(z_typed, band_inverse, ld_untyped, trait_mix, win_start, win_count):
    trait_cols = z_typed.shape[1]
    typed_blocks = z_typed.shape[0] // BLK
    padded = padded_2(z_typed, ((("sec", "var"), 0),), BLK)
    stacked = jnp.concatenate(
        [
            padded[k * BLK : (k + typed_blocks) * BLK].reshape(typed_blocks, BLK, trait_cols)
            for k in range(3)
        ],
        axis=1,
    )
    whitened = jnp.einsum(
        "bij,bjc->bic", band_inverse, stacked, preferred_element_type=jnp.float32
    ).astype(jnp.bfloat16)
    whitened_rows = whitened.reshape(typed_blocks * BLK, trait_cols)
    column_start = lax.axis_index("trait") * trait_cols
    mix_cols = lax.dynamic_slice_in_dim(trait_mix, column_start, trait_cols, 1)
    mixed_sums = jnp.dot(
        lax.all_gather(whitened_rows, "trait", axis=1, tiled=True),
        mix_cols,
        preferred_element_type=jnp.float32,
    )
    mixed = mixed_sums.astype(jnp.bfloat16).reshape(typed_blocks, BLK, trait_cols)
    window_steps = jnp.arange(WIN, dtype=jnp.int32)
    usable = window_steps[None, :] < win_count[:, None]
    untyped_blocks = win_start.shape[0]
    extended = padded_2(mixed, ((("sec", "var"), 0),), typed_blocks)
    local_first = win_start - lax.axis_index(("sec", "var")) * typed_blocks + typed_blocks
    wanted = jnp.clip(local_first[:, None] + window_steps[None, :], 0, 3 * typed_blocks - 1)
    picked = extended[wanted]
    chosen = jnp.where(usable[:, :, None, None], picked, jnp.zeros_like(picked))
    window_rows = chosen.reshape(untyped_blocks, WIN * BLK, trait_cols)
    imputed = jnp.einsum(
        "uij,ujc->uic", ld_untyped, window_rows, preferred_element_type=jnp.float32
    ).astype(jnp.bfloat16)
    return imputed.reshape(untyped_blocks * BLK, trait_cols)


def solution(mesh):
    in_specs = (
        P(("sec", "var"), "trait"),
        P(("sec", "var"), None, None),
        P(("sec", "var"), None, None),
        P(),
        P(("sec", "var")),
        P(("sec", "var")),
    )
    out_specs = P(("sec", "var"), "trait")
    return jax.shard_map(
        on_device, mesh=mesh, in_specs=in_specs, out_specs=out_specs, check_vma=False
    )
```

profile of v0, /device:TPU:24, one launch (start us, length us, event | category | flops | bytes accessed | tf_op | source)
XLA Modules:
  0.0 152.1 jit_solution(10747132638285355354)
XLA Ops:
  6.5 0.0 copy-start
  6.5 0.0 all-gather.2.cloned.1.call-start
  6.5 0.9 fusion.12
  7.5 3.9 %collective-permute-start = (bf16[128,128]{1,0:T(8,128)(2,1)S(1)}, bf16[128,128]{1,0:T(8,128)(2,1)S(1)}, u32[]{:S(2)}, u32[]{:S(2)}) collective-permute-start(bf16[128,128]{1,0:T(8,128)(2,1)S(1)} %get-tuple-element.7), channel_id=1, source_target_pairs={{0,4},{4,8},{8,12},{12,16},{16,20},{20,24},{24,28},{28,32},{32,36}... | collective-permute-start | bytes 98312 | tf_op jit(solution)/shard_map/ppermute | solution.py:18
  11.4 6.0 %collective-permute-start.1 = (bf16[128,128]{1,0:T(8,128)(2,1)S(1)}, bf16[128,128]{1,0:T(8,128)(2,1)S(1)}, u32[]{:S(2)}, u32[]{:S(2)}) collective-permute-start(bf16[128,128]{1,0:T(8,128)(2,1)S(1)} %get-tuple-element.8), channel_id=1, source_target_pairs={{4,0},{8,4},{12,8},{16,12},{20,16},{24,20},{28,24},{32,28},{36,32}... | collective-permute-start | bytes 98312 | tf_op jit(solution)/shard_map/ppermute | solution.py:20
  17.5 0.0 collective-permute-done
  17.5 1.6 %collective-permute-done.1 = bf16[128,128]{1,0:T(8,128)(2,1)S(1)} collective-permute-done((bf16[128,128]{1,0:T(8,128)(2,1)S(1)}, bf16[128,128]{1,0:T(8,128)(2,1)S(1)}, u32[]{:S(2)}, u32[]{:S(2)}) %collective-permute-start.1) | collective-permute-done | bytes 32800 | tf_op jit(solution)/shard_map/ppermute | solution.py:20
  19.0 1.7 %pad_maximum_fusion.2 = (bf16[4096,128]{1,0:T(8,128)(2,1)S(1)}, bf16[4096,128]{1,0:T(8,128)(2,1)S(1)}) fusion(bf16[4096,128]{1,0:T(8,128)(2,1)} %param.6, bf16[128,128]{1,0:T(8,128)(2,1)S(1)} %collective-permute-done, bf16[128,128]{1,0:T(8,128)(2,1)S(1)} %collective-permute-done.1), kind=kLoop, calls=%fused_computation.13 | loop fusion | flops 4194304 | bytes 3211264 | tf_op jit(solution)/shard_map/concatenate | solution.py:16
  20.8 3.2 %fusion.6 = bf16[32,128,128]{1,2,0:T(8,128)(2,1)} fusion(bf16[32,128,384]{2,1,0:T(8,128)(2,1)S(1)} %copy-done, bf16[32,128,128]{2,1,0:T(8,128)(2,1)S(1)} %bitcast.26, bf16[32,128,128]{2,1,0:T(8,128)(2,1)} %bitcast.24, bf16[32,128,128]{2,1,0:T(8,128)(2,1)S(1)} %bitcast.25), kind=kOutput, calls=%fused_computation.11 | convolution fusion | flops 412614656 | bytes 7340032 | tf_op jit(solution)/shard_map/bij,bjc->bic/dot_general | solution.py:38
  24.0 0.0 all-gather.2.cloned.1.call-update
  24.0 55.4 %all-gather.2.cloned.1.call-done = bf16[4096,512]{1,0:T(8,128)(2,1)} async-done(((bf16[4096,128]{1,0:T(8,128)(2,1)}), bf16[4096,512]{1,0:T(8,128)(2,1)}) %all-gather.2.cloned.1.call-update) | async-done | bytes 4194320 | tf_op jit(solution)/shard_map/all_gather | solution.py:45
  79.4 4.4 %convolution_convert_fusion = bf16[4096,128]{1,0:T(8,128)(2,1)} fusion(bf16[4096,512]{1,0:T(8,128)(2,1)} %all-gather.2.cloned.1.call-done, bf16[512,512]{1,0:T(8,128)(2,1)} %param.9, s32[]{:T(128)S(6)} %select_n.18), kind=kOutput, calls=%fused_computation.2 | convolution fusion | flops 537395200 | bytes 5373956 | tf_op jit(solution)/shard_map/dot_general | solution.py:44
  83.8 5.5 %collective-permute-start.3 = (bf16[32,128,128]{2,1,0:T(8,128)(2,1)}, bf16[32,128,128]{2,1,0:T(8,128)(2,1)}, u32[]{:S(2)}, u32[]{:S(2)}) collective-permute-start(bf16[32,128,128]{2,1,0:T(8,128)(2,1)} %bitcast.5), channel_id=1, source_target_pairs={{4,0},{8,4},{12,8},{16,12},{20,16},{24,20},{28,24},{32,28},{36,32}... | collective-permute-start | bytes 3145736 | tf_op jit(solution)/shard_map/ppermute | solution.py:20
  89.3 1.9 %collective-permute-start.2 = (bf16[32,128,128]{2,1,0:T(8,128)(2,1)}, bf16[32,128,128]{2,1,0:T(8,128)(2,1)}, u32[]{:S(2)}, u32[]{:S(2)}) collective-permute-start(bf16[32,128,128]{2,1,0:T(8,128)(2,1)} %bitcast.5), channel_id=1, source_target_pairs={{0,4},{4,8},{8,12},{12,16},{16,20},{20,24},{24,28},{28,32},{32,36}... | collective-permute-start | bytes 3145736 | tf_op jit(solution)/shard_map/ppermute | solution.py:18
  91.3 0.1 iota_compare_fusion
  91.4 0.1 broadcast_in_dim.21
  91.5 0.1 compare_select_fusion
  91.6 0.1 reshape.93
  91.8 19.4 %collective-permute-done.3 = bf16[32,128,128]{2,1,0:T(8,128)(2,1)} collective-permute-done((bf16[32,128,128]{2,1,0:T(8,128)(2,1)}, bf16[32,128,128]{2,1,0:T(8,128)(2,1)}, u32[]{:S(2)}, u32[]{:S(2)}) %collective-permute-start.3) | collective-permute-done | bytes 1048608 | tf_op jit(solution)/shard_map/ppermute | solution.py:20
  111.2 6.2 %collective-permute-done.2 = bf16[32,128,128]{2,1,0:T(8,128)(2,1)} collective-permute-done((bf16[32,128,128]{2,1,0:T(8,128)(2,1)}, bf16[32,128,128]{2,1,0:T(8,128)(2,1)}, u32[]{:S(2)}, u32[]{:S(2)}) %collective-permute-start.2) | collective-permute-done | bytes 1048608 | tf_op jit(solution)/shard_map/ppermute | solution.py:18
  117.4 3.3 %pad_maximum_fusion = bf16[96,128,128]{2,1,0:T(8,128)(2,1)} fusion(bf16[32,128,128]{2,1,0:T(8,128)(2,1)} %collective-permute-done.3, bf16[32,128,128]{2,1,0:T(8,128)(2,1)} %bitcast.5, bf16[32,128,128]{2,1,0:T(8,128)(2,1)} %collective-permute-done.2), kind=kLoop, calls=%fused_computation.9 | loop fusion | flops 3145728 | bytes 6291456 | tf_op jit(solution)/shard_map/concatenate | solution.py:16
  120.7 10.5 %gather_fusion = bf16[256,128,128]{2,1,0:T(8,128)(2,1)} fusion(bf16[96,128,128]{2,1,0:T(8,128)(2,1)} %pad_maximum_fusion, s32[1024]{0:T(1024)S(1)} %pad_clamp_fusion), kind=kCustom, calls=%fused_computation | custom fusion | bytes 16778240 | tf_op jit(solution)/shard_map/gather | solution.py:56
  131.2 7.0 %bitcast_select_fusion = bf16[64,512,128]{2,1,0:T(8,128)(2,1)S(1)} fusion(pred[64,512]{1,0:T(8,128)(4,1)S(1)} %bitcast.28, bf16[64,512,128]{2,1,0:T(8,128)(2,1)} %bitcast.23), kind=kLoop, calls=%fused_computation.1 | loop fusion | flops 4194304 | bytes 16809984 | tf_op jit(solution)/shard_map/jit(_where)/select_n | solution.py:57
  138.2 7.0 %convolution_convert_fusion.1 = bf16[64,128,128]{1,2,0:T(8,128)(2,1)} fusion(bf16[64,128,512]{2,1,0:T(8,128)(2,1)} %param.8, bf16[64,512,128]{2,1,0:T(8,128)(2,1)S(1)} %bitcast_select_fusion), kind=kOutput, calls=%fused_computation.10 | convolution fusion | flops 1074790400 | bytes 18874368 | tf_op jit(solution)/shard_map/uij,ujc->uic/dot_general | solution.py:59
  (8 shorter events, 0.0 us)
Async XLA Ops:
  6.5 14.2 %copy-start = (bf16[32,128,384]{2,1,0:T(8,128)(2,1)S(1)}, bf16[32,128,384]{2,1,0:T(8,128)(2,1)}, u32[]{:S(2)}) copy-start(bf16[32,128,384]{2,1,0:T(8,128)(2,1)} %param.7) | copy-start | bytes 9437188
  6.5 72.9 %all-gather.2.cloned.1.call-start = ((), (), s32[]{:S(2)}) async-start(), calls=%async_computation | async-start | bytes 5242880 | tf_op jit(solution)/shard_map/all_gather | solution.py:45
  7.5 10.0 %collective-permute-start = (bf16[128,128]{1,0:T(8,128)(2,1)S(1)}, bf16[128,128]{1,0:T(8,128)(2,1)S(1)}, u32[]{:S(2)}, u32[]{:S(2)}) collective-permute-start(bf16[128,128]{1,0:T(8,128)(2,1)S(1)} %get-tuple-element.7), channel_id=1, source_target_pairs={{0,4},{4,8},{8,12},{12,16},{16,20},{20,24},{24,28},{28,32},{32,36}... | collective-permute-start | bytes 98312 | tf_op jit(solution)/shard_map/ppermute | solution.py:18
  11.4 7.6 %collective-permute-start.1 = (bf16[128,128]{1,0:T(8,128)(2,1)S(1)}, bf16[128,128]{1,0:T(8,128)(2,1)S(1)}, u32[]{:S(2)}, u32[]{:S(2)}) collective-permute-start(bf16[128,128]{1,0:T(8,128)(2,1)S(1)} %get-tuple-element.8), channel_id=1, source_target_pairs={{4,0},{8,4},{12,8},{16,12},{20,16},{24,20},{28,24},{32,28},{36,32}... | collective-permute-start | bytes 98312 | tf_op jit(solution)/shard_map/ppermute | solution.py:20
  24.0 67.3 %copy-start.1 = (s32[64]{0:T(128)S(1)}, s32[64]{0:T(128)}, u32[]{:S(2)}) copy-start(s32[64]{0:T(128)} %param.11) | copy-start | bytes 772
  24.0 67.5 %copy-start.2 = (s32[64]{0:T(128)S(1)}, s32[64]{0:T(128)}, u32[]{:S(2)}) copy-start(s32[64]{0:T(128)} %param.10) | copy-start | bytes 772
  83.8 27.3 %collective-permute-start.3 = (bf16[32,128,128]{2,1,0:T(8,128)(2,1)}, bf16[32,128,128]{2,1,0:T(8,128)(2,1)}, u32[]{:S(2)}, u32[]{:S(2)}) collective-permute-start(bf16[32,128,128]{2,1,0:T(8,128)(2,1)} %bitcast.5), channel_id=1, source_target_pairs={{4,0},{8,4},{12,8},{16,12},{20,16},{24,20},{28,24},{32,28},{36,32}... | collective-permute-start | bytes 3145736 | tf_op jit(solution)/shard_map/ppermute | solution.py:20
  89.3 28.1 %collective-permute-start.2 = (bf16[32,128,128]{2,1,0:T(8,128)(2,1)}, bf16[32,128,128]{2,1,0:T(8,128)(2,1)}, u32[]{:S(2)}, u32[]{:S(2)}) collective-permute-start(bf16[32,128,128]{2,1,0:T(8,128)(2,1)} %bitcast.5), channel_id=1, source_target_pairs={{0,4},{4,8},{8,12},{12,16},{16,20},{20,24},{24,28},{28,32},{32,36}... | collective-permute-start | bytes 3145736 | tf_op jit(solution)/shard_map/ppermute | solution.py:18
Sparse Core Ops, SparseCore 0:
  24.1 55.2 all-gather.1
where the time goes:
time: 152 us
  waiting for transfers between devices  82.6 us (54%)
  starting transfers between devices  17.4 us (11%)
  matrix products  14.7 us (10%)
  between operations  13.5 us (9%)
  other arithmetic  12.2 us (8%)
  local copies, waits for them, and re-layouts  11.7 us (8%)
    all_gather x1, waiting for transfers between devices, on_device(): lax.all_gather(whitened_rows, 'trait', axis=1, tiled=True)  55.4 us
    ppermute x2, waiting for transfers between devices, padded_2(): lax.ppermute(head, axis, [((i + 1) % count, i) for i in range(ends)])  21 us
    ppermute x2, starting transfers between devices, padded_2(): lax.ppermute(head, axis, [((i + 1) % count, i) for i in range(ends)])  11.5 us
    gather x1, local copies, waits for them, and re-layouts, on_device(): picked = extended[wanted]  10.5 us
    dot_general x1, matrix products, on_device(): jnp.einsum('uij,ujc->uic', ld_untyped, window_rows, preferred_element_typ...  7.04 us
    select_n x1, other arithmetic, on_device(): chosen = jnp.where(usable[:, :, None, None], picked, jnp.zeros_like(picked))  7.01 us
    ppermute x2, waiting for transfers between devices, padded_2(): lax.ppermute(tail, axis, [(i, (i + 1) % count) for i in range(ends)])  6.23 us
    ppermute x2, starting transfers between devices, padded_2(): lax.ppermute(tail, axis, [(i, (i + 1) % count) for i in range(ends)])  5.87 us
  transfers between devices with their start and end apart: 5, of which 4 were waited for; matrix products, arithmetic and copies ran while one was open for 0% of the time, Pallas kernels for 0%

commit v1 on v0

--- a/solution.py
+++ b/solution.py
@@ -5,6 +5,27 @@
 
 BLK = 128
 WIN = 4
+
+
+def ring_gather(value, axis, dim):
+    length, position, extent = (lax.axis_size(axis), lax.axis_index(axis), value.shape[dim])
+    right = [(i, (i + 1) % length) for i in range(length)]
+    downward = [(i, (i - 1) % length) for i in range(length)]
+    whole = jnp.zeros((*value.shape[:dim], length * extent, *value.shape[dim + 1 :]), value.dtype)
+    whole = lax.dynamic_update_slice_in_dim(whole, value, position * extent, axis=dim)
+    from_left = from_right = value
+    middle = length // 2
+    for step in range(1, middle + 1):
+        from_left = lax.ppermute(from_left, axis, right)
+        whole = lax.dynamic_update_slice_in_dim(
+            whole, from_left, (position - step) % length * extent, axis=dim
+        )
+        if step < length - middle:
+            from_right = lax.ppermute(from_right, axis, downward)
+            whole = lax.dynamic_update_slice_in_dim(
+                whole, from_right, (position + step) % length * extent, axis=dim
+            )
+    return whole
 
 
 def padded_2(cells, sides, width):
@@ -42,9 +63,7 @@
     column_start = lax.axis_index("trait") * trait_cols
     mix_cols = lax.dynamic_slice_in_dim(trait_mix, column_start, trait_cols, 1)
     mixed_sums = jnp.dot(
-        lax.all_gather(whitened_rows, "trait", axis=1, tiled=True),
-        mix_cols,
-        preferred_element_type=jnp.float32,
+        ring_gather(whitened_rows, "trait", 1), mix_cols, preferred_element_type=jnp.float32
     )
     mixed = mixed_sums.astype(jnp.bfloat16).reshape(typed_blocks, BLK, trait_cols)
     window_steps = jnp.arange(WIN, dtype=jnp.int32)

time: 152 us -> 131 us (0.86)
  waiting for transfers between devices: 82.6 us -> 66.8 us
  between operations: 13.5 us -> 0.17 us
  local copies, waits for them, and re-layouts: 11.7 us -> 16.7 us
  starting transfers between devices: 17.4 us -> 21.3 us
    all_gather x1 -> x0, waiting for transfers between devices: 55.4 us -> none  [on_device(): lax.all_gather(whitened_rows, 'trait', axis=1, tiled=True)]
    ppermute x0 -> x3, waiting for transfers between devices: none -> 41.9 us  [the longest x2 41.9 us: ring_gather(): from_left = lax.ppermute(from_left, axis, right)]
    dynamic_update_slice x0 -> x4, local copies, waits for them, and re-layouts: none -> 4.69 us  [the longest x2 1.73 us: ring_gather(): lax.dynamic_update_slice_in_dim(whole, from_left, (position - step) % len...]
    ppermute x0 -> x3, starting transfers between devices: none -> 3.51 us  [the longest x2 1.77 us: ring_gather(): from_left = lax.ppermute(from_left, axis, right)]
    ppermute x2, waiting for transfers between devices: 21 us -> 18.7 us  [padded_2(): lax.ppermute(head, axis, [((i + 1) % count, i) for i in range(ends)])]
  transfers between devices with their start and end apart: 5 -> 7, of which waited for: 4 -> 5; matrix products, arithmetic and copies ran while one was open for 0% -> 4% of each run, Pallas kernels for 0% -> 0%
where the time goes in v1:
time: 131 us; the launch traced here: 130 us
  waiting for transfers between devices  66.8 us (51%)
  starting transfers between devices  21.3 us (16%)
  local copies, waits for them, and re-layouts  16.7 us (13%)
  matrix products  13.4 us (10%)
  other arithmetic  12.2 us (9%)
    ppermute x2, waiting for transfers between devices, ring_gather(): from_left = lax.ppermute(from_left, axis, right)  41.9 us
    ppermute x2, waiting for transfers between devices, padded_2(): lax.ppermute(head, axis, [((i + 1) % count, i) for i in range(ends)])  18.7 us
    ppermute x2, starting transfers between devices, padded_2(): lax.ppermute(head, axis, [((i + 1) % count, i) for i in range(ends)])  11.8 us
    gather x1, local copies, waits for them, and re-layouts, on_device(): picked = extended[wanted]  10.5 us
    dot_general x1, matrix products, on_device(): jnp.einsum('uij,ujc->uic', ld_untyped, window_rows, preferred_element_typ...  7.04 us
    select_n x1, other arithmetic, on_device(): chosen = jnp.where(usable[:, :, None, None], picked, jnp.zeros_like(picked))  7.01 us
    ppermute x2, waiting for transfers between devices, padded_2(): lax.ppermute(tail, axis, [(i, (i + 1) % count) for i in range(ends)])  6.23 us
    ppermute x2, starting transfers between devices, padded_2(): lax.ppermute(tail, axis, [(i, (i + 1) % count) for i in range(ends)])  6.05 us
  transfers between devices with their start and end apart: 7, of which 5 were waited for; matrix products, arithmetic and copies ran while one was open for 4% of the time, Pallas kernels for 0%

profile of v1, /device:TPU:24, one launch (start us, length us, event | category | flops | bytes accessed | tf_op | source)
XLA Modules:
  0.0 130.5 jit_solution(10135638704301811702)
XLA Ops:
  0.0 0.9 fusion.12
  0.9 3.9 %collective-permute-start = (bf16[128,128]{1,0:T(8,128)(2,1)S(1)}, bf16[128,128]{1,0:T(8,128)(2,1)S(1)}, u32[]{:S(2)}, u32[]{:S(2)}) collective-permute-start(bf16[128,128]{1,0:T(8,128)(2,1)S(1)} %get-tuple-element.7), channel_id=1, source_target_pairs={{0,4},{4,8},{8,12},{12,16},{16,20},{20,24},{24,28},{28,32},{32,36}... | collective-permute-start | bytes 98312 | tf_op jit(solution)/shard_map/ppermute | solution.py:39
  4.9 6.0 %collective-permute-start.1 = (bf16[128,128]{1,0:T(8,128)(2,1)S(1)}, bf16[128,128]{1,0:T(8,128)(2,1)S(1)}, u32[]{:S(2)}, u32[]{:S(2)}) collective-permute-start(bf16[128,128]{1,0:T(8,128)(2,1)S(1)} %get-tuple-element.8), channel_id=1, source_target_pairs={{4,0},{8,4},{12,8},{16,12},{20,16},{24,20},{28,24},{32,28},{36,32}... | collective-permute-start | bytes 98312 | tf_op jit(solution)/shard_map/ppermute | solution.py:41
  10.9 1.6 %collective-permute-done.1 = bf16[128,128]{1,0:T(8,128)(2,1)S(1)} collective-permute-done((bf16[128,128]{1,0:T(8,128)(2,1)S(1)}, bf16[128,128]{1,0:T(8,128)(2,1)S(1)}, u32[]{:S(2)}, u32[]{:S(2)}) %collective-permute-start.1) | collective-permute-done | bytes 32800 | tf_op jit(solution)/shard_map/ppermute | solution.py:41
  12.5 1.7 %pad_maximum_fusion.2 = (bf16[4096,128]{1,0:T(8,128)(2,1)S(1)}, bf16[4096,128]{1,0:T(8,128)(2,1)S(1)}) fusion(bf16[4096,128]{1,0:T(8,128)(2,1)} %param.6, bf16[128,128]{1,0:T(8,128)(2,1)S(1)} %collective-permute-done, bf16[128,128]{1,0:T(8,128)(2,1)S(1)} %collective-permute-done.1), kind=kLoop, calls=%fused_computation.13 | loop fusion | flops 4194304 | bytes 3211264 | tf_op jit(solution)/shard_map/concatenate | solution.py:37
  14.2 3.2 %fusion.6 = bf16[32,128,128]{1,2,0:T(8,128)(2,1)} fusion(bf16[32,128,384]{2,1,0:T(8,128)(2,1)S(1)} %copy-done, bf16[32,128,128]{2,1,0:T(8,128)(2,1)S(1)} %bitcast.26, bf16[32,128,128]{2,1,0:T(8,128)(2,1)} %bitcast.24, bf16[32,128,128]{2,1,0:T(8,128)(2,1)S(1)} %bitcast.25), kind=kOutput, calls=%fused_computation.11 | convolution fusion | flops 412614656 | bytes 7340032 | tf_op jit(solution)/shard_map/bij,bjc->bic/dot_general | solution.py:59
  17.4 1.5 %collective-permute-start.2 = (bf16[4096,128]{1,0:T(8,128)(2,1)}, bf16[4096,128]{1,0:T(8,128)(2,1)}, u32[]{:S(2)}, u32[]{:S(2)}) collective-permute-start(bf16[4096,128]{1,0:T(8,128)(2,1)} %bitcast.4), channel_id=1, source_target_pairs={{0,1},{1,2},{2,3},{3,0},{4,5},{5,6},{6,7},{7,4},{8,9},{9,10},{10,1... | collective-permute-start | bytes 3145736 | tf_op jit(solution)/shard_map/ppermute | solution.py:19
  18.9 1.7 %collective-permute-start.3 = (bf16[4096,128]{1,0:T(8,128)(2,1)}, bf16[4096,128]{1,0:T(8,128)(2,1)}, u32[]{:S(2)}, u32[]{:S(2)}) collective-permute-start(bf16[4096,128]{1,0:T(8,128)(2,1)} %bitcast.4), channel_id=1, source_target_pairs={{0,3},{1,0},{2,1},{3,2},{4,7},{5,4},{6,5},{7,6},{8,11},{9,8},{10,9... | collective-permute-start | bytes 3145736 | tf_op jit(solution)/shard_map/ppermute | solution.py:24
  20.7 22.3 %collective-permute-done.2 = bf16[4096,128]{1,0:T(8,128)(2,1)} collective-permute-done((bf16[4096,128]{1,0:T(8,128)(2,1)}, bf16[4096,128]{1,0:T(8,128)(2,1)}, u32[]{:S(2)}, u32[]{:S(2)}) %collective-permute-start.2) | collective-permute-done | bytes 1048608 | tf_op jit(solution)/shard_map/ppermute | solution.py:19
  43.0 0.3 collective-permute-start.4
  43.3 0.3 broadcast_in_dim.27
  43.6 1.5 %constant_dynamic-update-slice_fusion.3 = bf16[4096,512]{1,0:T(8,128)(2,1)S(1)} fusion(bf16[4096,512]{1,0:T(8,128)(2,1)S(1)} %broadcast_in_dim.27, bf16[4096,128]{1,0:T(8,128)(2,1)} %bitcast.4, s32[]{:T(128)S(6)} %select_n.43), kind=kLoop, calls=%fused_computation.23 | loop fusion | bytes 2097156 | tf_op jit(solution)/shard_map/dynamic_update_slice | solution.py:15
  45.1 1.5 %constant_dynamic-update-slice_fusion.2 = bf16[4096,512]{1,0:T(8,128)(2,1)S(1)} fusion(bf16[4096,512]{1,0:T(8,128)(2,1)S(1)} %constant_dynamic-update-slice_fusion.3, bf16[4096,128]{1,0:T(8,128)(2,1)} %collective-permute-done.2, s32[]{:T(128)S(6)} %select_n.45), kind=kLoop, calls=%fused_computation.22 | loop fusion | bytes 2097156 | tf_op jit(solution)/shard_map/dynamic_update_slice | solution.py:20
  46.5 1.5 %constant_dynamic-update-slice_fusion.1 = bf16[4096,512]{1,0:T(8,128)(2,1)S(1)} fusion(bf16[4096,512]{1,0:T(8,128)(2,1)S(1)} %constant_dynamic-update-slice_fusion.2, bf16[4096,128]{1,0:T(8,128)(2,1)} %collective-permute-done.3, s32[]{:T(128)S(6)} %select_n.47), kind=kLoop, calls=%fused_computation.21 | loop fusion | bytes 2097156 | tf_op jit(solution)/shard_map/dynamic_update_slice | solution.py:25
  48.1 19.5 %collective-permute-done.4 = bf16[4096,128]{1,0:T(8,128)(2,1)S(1)} collective-permute-done((bf16[4096,128]{1,0:T(8,128)(2,1)}, bf16[4096,128]{1,0:T(8,128)(2,1)S(1)}, u32[]{:S(2)}, u32[]{:S(2)}) %collective-permute-start.4) | collective-permute-done | bytes 1048608 | tf_op jit(solution)/shard_map/ppermute | solution.py:19
  67.8 3.1 %convolution_convert_fusion = bf16[4096,128]{1,0:T(8,128)(2,1)} fusion(bf16[4096,512]{1,0:T(8,128)(2,1)S(1)} %constant_dynamic-update-slice_fusion, bf16[512,512]{1,0:T(8,128)(2,1)} %param.9, s32[]{:T(128)S(6)} %select_n.43), kind=kOutput, calls=%fused_computation.2 | convolution fusion | flops 537395200 | bytes 5373956 | tf_op jit(solution)/shard_map/dot_general | solution.py:65
  71.0 5.7 %collective-permute-start.6 = (bf16[32,128,128]{2,1,0:T(8,128)(2,1)}, bf16[32,128,128]{2,1,0:T(8,128)(2,1)}, u32[]{:S(2)}, u32[]{:S(2)}) collective-permute-start(bf16[32,128,128]{2,1,0:T(8,128)(2,1)} %bitcast.6), channel_id=1, source_target_pairs={{4,0},{8,4},{12,8},{16,12},{20,16},{24,20},{28,24},{32,28},{36,32}... | collective-permute-start | bytes 3145736 | tf_op jit(solution)/shard_map/ppermute | solution.py:41
  76.7 2.1 %collective-permute-start.5 = (bf16[32,128,128]{2,1,0:T(8,128)(2,1)}, bf16[32,128,128]{2,1,0:T(8,128)(2,1)}, u32[]{:S(2)}, u32[]{:S(2)}) collective-permute-start(bf16[32,128,128]{2,1,0:T(8,128)(2,1)} %bitcast.6), channel_id=1, source_target_pairs={{0,4},{4,8},{8,12},{12,16},{16,20},{20,24},{24,28},{28,32},{32,36}... | collective-permute-start | bytes 3145736 | tf_op jit(solution)/shard_map/ppermute | solution.py:39
  79.3 17.1 %collective-permute-done.6 = bf16[32,128,128]{2,1,0:T(8,128)(2,1)} collective-permute-done((bf16[32,128,128]{2,1,0:T(8,128)(2,1)}, bf16[32,128,128]{2,1,0:T(8,128)(2,1)}, u32[]{:S(2)}, u32[]{:S(2)}) %collective-permute-start.6) | collective-permute-done | bytes 1048608 | tf_op jit(solution)/shard_map/ppermute | solution.py:41
  96.4 6.2 %collective-permute-done.5 = bf16[32,128,128]{2,1,0:T(8,128)(2,1)} collective-permute-done((bf16[32,128,128]{2,1,0:T(8,128)(2,1)}, bf16[32,128,128]{2,1,0:T(8,128)(2,1)}, u32[]{:S(2)}, u32[]{:S(2)}) %collective-permute-start.5) | collective-permute-done | bytes 1048608 | tf_op jit(solution)/shard_map/ppermute | solution.py:39
  102.6 3.3 %pad_maximum_fusion = bf16[96,128,128]{2,1,0:T(8,128)(2,1)} fusion(bf16[32,128,128]{2,1,0:T(8,128)(2,1)} %collective-permute-done.6, bf16[32,128,128]{2,1,0:T(8,128)(2,1)} %bitcast.6, bf16[32,128,128]{2,1,0:T(8,128)(2,1)} %collective-permute-done.5), kind=kLoop, calls=%fused_computation.9 | loop fusion | flops 3145728 | bytes 6291456 | tf_op jit(solution)/shard_map/concatenate | solution.py:37
  105.9 10.5 %gather_fusion = bf16[256,128,128]{2,1,0:T(8,128)(2,1)} fusion(bf16[96,128,128]{2,1,0:T(8,128)(2,1)} %pad_maximum_fusion, s32[1024]{0:T(1024)S(1)} %pad_clamp_fusion), kind=kCustom, calls=%fused_computation | custom fusion | bytes 16778240 | tf_op jit(solution)/shard_map/gather | solution.py:75
  116.4 7.0 %bitcast_select_fusion = bf16[64,512,128]{2,1,0:T(8,128)(2,1)S(1)} fusion(pred[64,512]{1,0:T(8,128)(4,1)S(1)} %bitcast.27, bf16[64,512,128]{2,1,0:T(8,128)(2,1)} %bitcast.23), kind=kLoop, calls=%fused_computation.1 | loop fusion | flops 4194304 | bytes 16809984 | tf_op jit(solution)/shard_map/jit(_where)/select_n | solution.py:76
  123.4 7.0 %convolution_convert_fusion.1 = bf16[64,128,128]{1,2,0:T(8,128)(2,1)} fusion(bf16[64,128,512]{2,1,0:T(8,128)(2,1)} %param.8, bf16[64,512,128]{2,1,0:T(8,128)(2,1)S(1)} %bitcast_select_fusion), kind=kOutput, calls=%fused_computation.10 | convolution fusion | flops 1074790400 | bytes 18874368 | tf_op jit(solution)/shard_map/uij,ujc->uic/dot_general | solution.py:78
  (16 shorter events, 0.7 us)
Async XLA Ops:
  0.0 14.2 %copy-start = (bf16[32,128,384]{2,1,0:T(8,128)(2,1)S(1)}, bf16[32,128,384]{2,1,0:T(8,128)(2,1)}, u32[]{:S(2)}) copy-start(bf16[32,128,384]{2,1,0:T(8,128)(2,1)} %param.7) | copy-start | bytes 9437188
  0.9 10.0 %collective-permute-start = (bf16[128,128]{1,0:T(8,128)(2,1)S(1)}, bf16[128,128]{1,0:T(8,128)(2,1)S(1)}, u32[]{:S(2)}, u32[]{:S(2)}) collective-permute-start(bf16[128,128]{1,0:T(8,128)(2,1)S(1)} %get-tuple-element.7), channel_id=1, source_target_pairs={{0,4},{4,8},{8,12},{12,16},{16,20},{20,24},{24,28},{28,32},{32,36}... | collective-permute-start | bytes 98312 | tf_op jit(solution)/shard_map/ppermute | solution.py:39
  4.9 7.6 %collective-permute-start.1 = (bf16[128,128]{1,0:T(8,128)(2,1)S(1)}, bf16[128,128]{1,0:T(8,128)(2,1)S(1)}, u32[]{:S(2)}, u32[]{:S(2)}) collective-permute-start(bf16[128,128]{1,0:T(8,128)(2,1)S(1)} %get-tuple-element.8), channel_id=1, source_target_pairs={{4,0},{8,4},{12,8},{16,12},{20,16},{24,20},{28,24},{32,28},{36,32}... | collective-permute-start | bytes 98312 | tf_op jit(solution)/shard_map/ppermute | solution.py:41
  17.4 25.6 %collective-permute-start.2 = (bf16[4096,128]{1,0:T(8,128)(2,1)}, bf16[4096,128]{1,0:T(8,128)(2,1)}, u32[]{:S(2)}, u32[]{:S(2)}) collective-permute-start(bf16[4096,128]{1,0:T(8,128)(2,1)} %bitcast.4), channel_id=1, source_target_pairs={{0,1},{1,2},{2,3},{3,0},{4,5},{5,6},{6,7},{7,4},{8,9},{9,10},{10,1... | collective-permute-start | bytes 3145736 | tf_op jit(solution)/shard_map/ppermute | solution.py:19
  18.9 27.6 %collective-permute-start.3 = (bf16[4096,128]{1,0:T(8,128)(2,1)}, bf16[4096,128]{1,0:T(8,128)(2,1)}, u32[]{:S(2)}, u32[]{:S(2)}) collective-permute-start(bf16[4096,128]{1,0:T(8,128)(2,1)} %bitcast.4), channel_id=1, source_target_pairs={{0,3},{1,0},{2,1},{3,2},{4,7},{5,4},{6,5},{7,6},{8,11},{9,8},{10,9... | collective-permute-start | bytes 3145736 | tf_op jit(solution)/shard_map/ppermute | solution.py:24
  43.0 24.5 %collective-permute-start.4 = (bf16[4096,128]{1,0:T(8,128)(2,1)}, bf16[4096,128]{1,0:T(8,128)(2,1)S(1)}, u32[]{:S(2)}, u32[]{:S(2)}) collective-permute-start(bf16[4096,128]{1,0:T(8,128)(2,1)} %collective-permute-done.2), channel_id=1, source_target_pairs={{0,1},{1,2},{2,3},{3,0},{4,5},{5,6},{6,7},{7,4},{8,9},{9,10},{10,1... | collective-permute-start | bytes 3145736 | tf_op jit(solution)/shard_map/ppermute | solution.py:19
  48.0 30.8 %copy-start.1 = (s32[64]{0:T(128)S(1)}, s32[64]{0:T(128)}, u32[]{:S(2)}) copy-start(s32[64]{0:T(128)} %param.11) | copy-start | bytes 772
  48.0 31.0 %copy-start.2 = (s32[64]{0:T(128)S(1)}, s32[64]{0:T(128)}, u32[]{:S(2)}) copy-start(s32[64]{0:T(128)} %param.10) | copy-start | bytes 772
  71.0 25.5 %collective-permute-start.6 = (bf16[32,128,128]{2,1,0:T(8,128)(2,1)}, bf16[32,128,128]{2,1,0:T(8,128)(2,1)}, u32[]{:S(2)}, u32[]{:S(2)}) collective-permute-start(bf16[32,128,128]{2,1,0:T(8,128)(2,1)} %bitcast.6), channel_id=1, source_target_pairs={{4,0},{8,4},{12,8},{16,12},{20,16},{24,20},{28,24},{32,28},{36,32}... | collective-permute-start | bytes 3145736 | tf_op jit(solution)/shard_map/ppermute | solution.py:41
  76.7 25.9 %collective-permute-start.5 = (bf16[32,128,128]{2,1,0:T(8,128)(2,1)}, bf16[32,128,128]{2,1,0:T(8,128)(2,1)}, u32[]{:S(2)}, u32[]{:S(2)}) collective-permute-start(bf16[32,128,128]{2,1,0:T(8,128)(2,1)} %bitcast.6), channel_id=1, source_target_pairs={{0,4},{4,8},{8,12},{12,16},{16,20},{20,24},{24,28},{28,32},{32,36}... | collective-permute-start | bytes 3145736 | tf_op jit(solution)/shard_map/ppermute | solution.py:39
